TPU v7x, 32 devices: a whole 2x2x4 slice. The times are simulated.
32 devices in a mesh: section: 4 (over z), seq: 4 (over y, x), tp: 2 (over core).
Axes of the slice: x: 2, y: 2, z: 4, core: 2. Of those that a mesh axis runs over, the one named last changes fastest.
Arguments:
- queries: bfloat16 [4, 1024, 8192], P('section', 'seq', 'tp'), may hold values from -300 to 300
- vision: bfloat16 [128, 7680], P(('section', 'tp'), 'seq'), may hold values from -6 to 6
- kv_weight: bfloat16 [4, 7680, 2048], P('section', 'seq', 'tp'), may hold values from -0.0625 to 0.0625
- key_gain: float32 [4, 128], P('section'), may hold values from 0.25 to 1.75
- head_gate: float32 [4, 64], P('section', 'tp'), may hold values from -1.5 to 1.5
Outputs:
- attended: bfloat16 [4, 1024, 8192], P('section', 'seq', 'tp')
All inputs are finite; a program needn't handle non-finite values.
Results may differ from a plain program's by a relative error of at most 0.01.
The roundings to bfloat16 on the way count: a program that leaves them out, or rounds other values in their place, can miss the bound.
Values may be sent and summed in bfloat16 or wider, within the bound.
A program may use at most 64 MiB of HBM per device.

v0:
```python
import math
import jax
import jax.numpy as jnp
from jax import lax
from jax.sharding import PartitionSpec as P

eps_norm = 1e-05


def normalize(projected, gain, head_dim):
    rows = projected.shape[0]
    shaped = projected.reshape(rows, -1, 2, head_dim)
    keys_raw = shaped[:, :, 0]
    values_raw = shaped[:, :, 1]
    scaled = (
        keys_raw
        * lax.rsqrt(jnp.mean(keys_raw * keys_raw, axis=-1, keepdims=True) + eps_norm)
        * gain
    )
    return (scaled.astype(jnp.bfloat16), values_raw.astype(jnp.bfloat16))


def fold_keys(carry, grouped, keys, values):
    rows = keys.shape[0]
    block = math.gcd(rows, 128)
    key_blocks = keys.reshape(rows // block, block, keys.shape[1], keys.shape[2])
    value_blocks = values.reshape(rows // block, block, values.shape[1], values.shape[2])
    scale = grouped.shape[-1] ** (-0.5)

    def advance(state, blocks):
        running_max, running_sum, weighted = state
        key_block, value_block = blocks
        scores = (
            jnp.einsum("tigd,rid->tigr", grouped, key_block, preferred_element_type=jnp.float32)
            * scale
        )
        new_max = jnp.maximum(running_max, jnp.max(scores, axis=-1))
        factor = jnp.exp(running_max - new_max)
        exp_scores = jnp.exp(scores - new_max[..., None])
        running_sum = running_sum * factor + jnp.sum(exp_scores, axis=-1)
        weighted = weighted * factor[..., None] + jnp.einsum(
            "tigr,rid->tigd",
            exp_scores.astype(jnp.bfloat16),
            value_block,
            preferred_element_type=jnp.float32,
        )
        return ((new_max, running_sum, weighted), None)

    state, unused = lax.scan(advance, carry, (key_blocks, value_blocks))
    return state


def local(queries, vision, kv_weight, key_gain, head_gate):
    local_weight = kv_weight[0]
    head_dim = key_gain.shape[1]
    partials = jnp.dot(
        lax.all_gather(vision, ("section", "tp"), axis=0, tiled=True),
        local_weight,
        preferred_element_type=jnp.float32,
    )
    tokens = queries.shape[1]
    pair_heads = local_weight.shape[1] // (2 * head_dim)
    query_heads = head_gate.shape[1]
    group = query_heads // pair_heads
    grouped = queries[0].reshape(tokens, pair_heads, group, head_dim)
    initial = (
        jnp.full((tokens, pair_heads, group), -1e30, jnp.float32),
        jnp.zeros((tokens, pair_heads, group), jnp.float32),
        jnp.zeros((tokens, pair_heads, group, head_dim), jnp.float32),
    )
    shares = lax.psum_scatter(partials, "seq", scatter_dimension=0, tiled=True)
    keys, values = normalize(shares, key_gain[0], head_dim)
    state = fold_keys(
        initial,
        grouped,
        lax.all_gather(keys, "seq", axis=0, tiled=True),
        lax.all_gather(values, "seq", axis=0, tiled=True),
    )
    running_max, running_sum, weighted = state
    gate = jnp.tanh(head_gate[0]).reshape(1, pair_heads, group, 1)
    result = weighted / running_sum[..., None] * gate
    return result.reshape(1, tokens, query_heads * head_dim).astype(jnp.bfloat16)


def solution(mesh):
    return jax.shard_map(
        local,
        mesh=mesh,
        in_specs=(
            P("section", "seq", "tp"),
            P(("section", "tp"), "seq"),
            P("section", "seq", "tp"),
            P("section", None),
            P("section", "tp"),
        ),
        out_specs=P("section", "seq", "tp"),
        check_vma=False,
    )
```

profile of v0, /device:TPU:0, one launch (start us, length us, event | category | flops | bytes accessed | tf_op | source)
XLA Modules:
  0.0 88.3 jit_solution(7843838622367598786)
XLA Ops:
  6.5 0.0 reduce-scatter.2.cloned.1.call-start
  6.5 16.7 %all_gather.9 = bf16[128,1920]{1,0:T(8,128)(2,1)S(1)} all-gather(bf16[16,1920]{1,0:T(8,128)(2,1)} %param.6), channel_id=1, replica_groups=mesh['section'=4,'seq'=4,'tp'=2] {'section','tp'}, dimensions={0}, use_global_device_ids=true | all-gather | bytes 552960 | tf_op jit(solution)/shard_map/all_gather | solution.py:57
  23.2 0.0 copy-start.2
  23.3 0.0 copy-start.1
  23.3 3.6 %fusion.4 = f32[128,1024]{1,0:T(8,128)} fusion(bf16[128,1920]{1,0:T(8,128)(2,1)S(1)} %all_gather.9, bf16[1,1920,1024]{2,1,0:T(8,128)(2,1)} %param.7), kind=kOutput, calls=%fused_computation.7 | convolution fusion | flops 503316480 | bytes 4947968 | tf_op jit(solution)/shard_map/dot_general | solution.py:56
  26.9 0.0 reduce-scatter.2.cloned.1.call-update
  26.9 2.1 %copy.22 = bf16[32,8,32,128]{3,2,1,0:T(8,128)(2,1)S(1)} copy(bf16[32,8,32,128]{3,1,2,0:T(8,128)(2,1)} %bitcast.48) | data formatting | bytes 4194304
  29.0 0.0 copy-done.2
  29.0 0.1 tanh.11
  29.1 24.1 %reduce-scatter.2.cloned.1.call-done = f32[32,1024]{1,0:T(8,128)} async-done(((f32[128,1024]{1,0:T(8,128)}), f32[32,1024]{1,0:T(8,128)}) %reduce-scatter.2.cloned.1.call-update) | async-done | bytes 131088 | tf_op jit(solution)/shard_map/reduce_scatter | solution.py:71
  53.2 1.0 %reshape.53 = f32[32,4,2,128]{3,2,1,0:T(2,128)S(1)} reshape(f32[32,1024]{1,0:T(8,128)} %reduce-scatter.2.cloned.1.call-done) | data formatting | bytes 262144 | tf_op jit(solution)/shard_map/reshape | solution.py:12
  54.3 0.1 slice.10
  54.4 0.1 multiply_reduce_fusion
  54.5 0.0 copy-done.1
  54.5 0.1 multiply_convert_fusion
  54.6 8.6 %all_gather.10 = bf16[128,4,128]{2,0,1:T(8,128)(2,1)S(1)} all-gather(bf16[32,4,128]{2,0,1:T(8,128)(2,1)S(1)} %multiply_convert_fusion), channel_id=1, replica_groups=mesh['section'=4,'seq'=4,'tp'=2] {'seq'}, dimensions={0}, use_global_device_ids=true | all-gather | bytes 163840 | tf_op jit(solution)/shard_map/all_gather | solution.py:76
  63.2 1.5 %bitcast_reduce_fusion = (f32[256,4,8]{0,2,1:T(8,128)S(1)}, f32[4,128,256,8]{2,1,3,0:T(8,128)S(1)}) fusion(bf16[256,4,8,128]{3,2,1,0:T(8,128)(2,1)S(1)} %bitcast.47, bf16[128,4,128]{2,0,1:T(8,128)(2,1)S(1)} %all_gather.10), kind=kOutput, calls=%fused_computation.5 | convolution fusion | flops 270524416 | bytes 6455296 | tf_op jit(solution)/shard_map/while/body/eval_jaxpr/tigd,rid->tigr/dot_general | solution.py:34
  64.7 0.0 copy-start
  64.7 1.9 %copy-done = f32[4,128,256,8]{2,1,3,0:T(8,128)} copy-done((f32[4,128,256,8]{2,1,3,0:T(8,128)}, f32[4,128,256,8]{2,1,3,0:T(8,128)S(1)}, u32[]{:S(2)}) %copy-start) | copy-done | bytes 4194328
  66.6 0.8 fusion.6
  67.5 7.3 %all-gather = bf16[128,4,1,128]{3,1,2,0:T(4,128)(2,1)S(1)} all-gather(bf16[32,4,1,128]{3,1,2,0:T(4,128)(2,1)S(1)} %copy.31), channel_id=2, replica_groups=mesh['section'=4,'seq'=4,'tp'=2] {'seq'}, dimensions={0}, use_global_device_ids=true | all-gather | bytes 163840 | tf_op jit(solution)/shard_map/all_gather | solution.py:77
  74.8 0.1 copy.14
  75.0 3.6 %fusion.2 = bf16[256,4,8,128]{0,3,2,1:T(8,128)(2,1)S(1)} fusion(f32[4,128,256,8]{2,1,3,0:T(8,128)} %copy-done, f32[4,8]{1,0:T(4,128)S(1)} %tanh.11, f32[256,4,8]{0,2,1:T(8,128)S(1)} %get-tuple-element.18, f32[256,4,8]{0,2,1:T(8,128)S(1)} %broadcast_maximum_fusion, f32[256,4,8]{0,2,1:T(8,128)S(1)} %get-tuple-element.17, bf16[128,4,1,128]{0,3,1,2:T(8,128)(2,1)S(1)} %copy.14), kind=kOutput, calls=%fused_computation.3 | convolution fusion | flops 275775488 | bytes 6520960 | tf_op jit(solution)/shard_map/while/body/eval_jaxpr/tigr,rid->tigd/dot_general | solution.py:41
  78.5 2.9 %copy.16 = bf16[1,256,4096]{2,1,0:T(8,128)(2,1)} copy(bf16[1,256,4096]{1,2,0:T(8,128)(2,1)S(1)} %bitcast.49) | data formatting | bytes 4194304 | tf_op jit(solution)/shard_map/convert_element_type | solution.py:82
  (6 shorter events, 0.1 us)
Async XLA Ops:
  6.5 46.7 %reduce-scatter.2.cloned.1.call-start = ((), (), s32[]{:S(2)}) async-start(), calls=%async_computation.1 | async-start | bytes 655360 | tf_op jit(solution)/shard_map/reduce_scatter | solution.py:71
  23.2 5.8 %copy-start.2 = (f32[1,32]{1,0:T(1,128)S(1)}, f32[1,32]{1,0:T(1,128)}, u32[]{:S(2)}) copy-start(f32[1,32]{1,0:T(1,128)} %param.9) | copy-start | bytes 388
  23.3 31.3 %copy-start.1 = (f32[1,128]{1,0:T(1,128)S(1)}, f32[1,128]{1,0:T(1,128)}, u32[]{:S(2)}) copy-start(f32[1,128]{1,0:T(1,128)} %param.8) | copy-start | bytes 1540
  64.7 1.9 %copy-start = (f32[4,128,256,8]{2,1,3,0:T(8,128)}, f32[4,128,256,8]{2,1,3,0:T(8,128)S(1)}, u32[]{:S(2)}) copy-start(f32[4,128,256,8]{2,1,3,0:T(8,128)S(1)} %get-tuple-element.20) | copy-start | bytes 12582916
Sparse Core Ops, SparseCore 0:
  27.0 26.1 reduce-scatter.1
where the time goes:
time: 88.5 us; the launch traced here: 88.3 us
  blocking collectives  32.6 us (37%)
  waiting for transfers between devices  24.1 us (27%)
  between operations  13.5 us (15%)
  matrix products  8.73 us (10%)
  local copies, waits for them, and re-layouts  8.23 us (9%)
  other arithmetic  1.01 us (1%)
    reduce_scatter x1, waiting for transfers between devices, local(): shares = lax.psum_scatter(partials, 'seq', scatter_dimension=0, tiled=True)  24.1 us
    all_gather x1, blocking collectives, local(): lax.all_gather(vision, ('section', 'tp'), axis=0, tiled=True)  16.7 us
    all_gather x1, blocking collectives, local(): lax.all_gather(keys, 'seq', axis=0, tiled=True)  8.61 us
    all_gather x1, blocking collectives, local(): lax.all_gather(values, 'seq', axis=0, tiled=True)  7.32 us
    unnamed x8, local copies, waits for them, and re-layouts  3.99 us
    dot_general x1, matrix products, local(): jnp.dot(lax.all_gather(vision, ('section', 'tp'), axis=0, tiled=True), lo...  3.65 us
    dot_general x1, matrix products, advance(): jnp.einsum('tigr,rid->tigd', exp_scores.astype(jnp.bfloat16), value_block...  3.58 us
    convert_element_type x1, local copies, waits for them, and re-layouts, local(): result.reshape(1, tokens, query_heads * head_dim).astype(jnp.bfloat16)  2.86 us
  transfers between devices with their start and end apart: 1, of which 1 were waited for; matrix products, arithmetic and copies ran while one was open for 2% of the time, Pallas kernels for 0%

commit v1 on v0

--- a/solution.py
+++ b/solution.py
@@ -5,6 +5,22 @@
 from jax.sharding import PartitionSpec as P
 
 eps_norm = 1e-05
+
+
+def ring_gather(x, axis, dim):
+    ways, here, step = (lax.axis_size(axis), lax.axis_index(axis), x.shape[dim])
+    shape = [n * ways if d == dim else n for d, n in enumerate(x.shape)]
+    full = lax.dynamic_update_slice_in_dim(jnp.zeros(shape, x.dtype), x, here * step, axis=dim)
+    going_up = going_down = x
+    for far in range(1, ways // 2 + 1):
+        going_up = lax.ppermute(going_up, axis, [(d, (d + 1) % ways) for d in range(ways)])
+        full = lax.dynamic_update_slice_in_dim(full, going_up, (here - far) % ways * step, axis=dim)
+        if 2 * far < ways:
+            going_down = lax.ppermute(going_down, axis, [(d, (d - 1) % ways) for d in range(ways)])
+            full = lax.dynamic_update_slice_in_dim(
+                full, going_down, (here + far) % ways * step, axis=dim
+            )
+    return full
 
 
 def normalize(projected, gain, head_dim):
@@ -54,9 +70,7 @@
     local_weight = kv_weight[0]
     head_dim = key_gain.shape[1]
     partials = jnp.dot(
-        lax.all_gather(vision, ("section", "tp"), axis=0, tiled=True),
-        local_weight,
-        preferred_element_type=jnp.float32,
+        ring_gather(vision, ("section", "tp"), 0), local_weight, preferred_element_type=jnp.float32
     )
     tokens = queries.shape[1]
     pair_heads = local_weight.shape[1] // (2 * head_dim)

time: 88.5 us -> 93 us (1.051)
  blocking collectives: 32.6 us -> 15.9 us
  starting transfers between devices: 0.01 us -> 11.8 us
  waiting for transfers between devices: 24.1 us -> 32.4 us
  local copies, waits for them, and re-layouts: 8.23 us -> 9.24 us
    all_gather x1 -> x0, blocking collectives: 16.7 us -> none  [local(): lax.all_gather(vision, ('section', 'tp'), axis=0, tiled=True)]
    ppermute x0 -> x7, starting transfers between devices: none -> 11.8 us  [the longest x3 11.3 us: ring_gather(): lax.ppermute(going_down, axis, [(d, (d - 1) % ways) for d in range(ways)])]
    ppermute x0 -> x7, waiting for transfers between devices: none -> 10.3 us  [the longest x4 9.58 us: ring_gather(): lax.ppermute(going_up, axis, [(d, (d + 1) % ways) for d in range(ways)])]
    reduce_scatter x1, waiting for transfers between devices: 24.1 us -> 22.1 us  [local(): shares = lax.psum_scatter(partials, 'seq', scatter_dimension=0, tiled=True)]
    dynamic_update_slice x0 -> x8, local copies, waits for them, and re-layouts: none -> 0.96 us  [the longest x1 0.87 us: ring_gather(): lax.dynamic_update_slice_in_dim(jnp.zeros(shape, x.dtype), x, here * step...]
  transfers between devices with their start and end apart: 1 -> 8, of which waited for: 1 -> 8; matrix products, arithmetic and copies ran while one was open for 2% -> 3% of each run, Pallas kernels for 0% -> 0%
where the time goes in v1:
time: 93 us; the launch traced here: 92.6 us
  waiting for transfers between devices  32.4 us (35%)
  blocking collectives  15.9 us (17%)
  between operations  13.5 us (15%)
  starting transfers between devices  11.8 us (13%)
  local copies, waits for them, and re-layouts  9.24 us (10%)
  matrix products  8.7 us (9%)
  other arithmetic  1.01 us (1%)
    reduce_scatter x1, waiting for transfers between devices, local(): shares = lax.psum_scatter(partials, 'seq', scatter_dimension=0, tiled=True)  22.1 us
    ppermute x3, starting transfers between devices, ring_gather(): lax.ppermute(going_down, axis, [(d, (d - 1) % ways) for d in range(ways)])  11.3 us
    ppermute x4, waiting for transfers between devices, ring_gather(): lax.ppermute(going_up, axis, [(d, (d + 1) % ways) for d in range(ways)])  9.58 us
    all_gather x1, blocking collectives, local(): lax.all_gather(keys, 'seq', axis=0, tiled=True)  8.61 us
    all_gather x1, blocking collectives, local(): lax.all_gather(values, 'seq', axis=0, tiled=True)  7.32 us
    unnamed x8, local copies, waits for them, and re-layouts  4.01 us
    dot_general x1, matrix products, local(): jnp.dot(ring_gather(vision, ('section', 'tp'), 0), local_weight, preferre...  3.63 us
    dot_general x1, matrix products, advance(): jnp.einsum('tigr,rid->tigd', exp_scores.astype(jnp.bfloat16), value_block...  3.58 us
  transfers between devices with their start and end apart: 8, of which 8 were waited for; matrix products, arithmetic and copies ran while one was open for 3% of the time, Pallas kernels for 0%

profile of v1, /device:TPU:0, one launch (start us, length us, event | category | flops | bytes accessed | tf_op | source)
XLA Modules:
  0.0 92.6 jit_solution(10795997631212306489)
XLA Ops:
  6.5 0.5 collective-permute-start
  7.0 4.0 %collective-permute-start.1 = (bf16[16,1920]{1,0:T(8,128)(2,1)}, bf16[16,1920]{1,0:T(8,128)(2,1)S(1)}, u32[]{:S(2)}, u32[]{:S(2)}) collective-permute-start(bf16[16,1920]{1,0:T(8,128)(2,1)} %param.6), channel_id=1, source_target_pairs={{0,25},{1,0},{8,1},{9,8},{16,9},{17,16},{24,17},{25,24},{2,27},{3,... | collective-permute-start | bytes 184328 | tf_op jit(solution)/shard_map/ppermute | solution.py:19
  11.1 0.9 constant_dynamic-update-slice_fusion.7
  12.0 1.2 %collective-permute-done = bf16[16,1920]{1,0:T(8,128)(2,1)S(1)} collective-permute-done((bf16[16,1920]{1,0:T(8,128)(2,1)}, bf16[16,1920]{1,0:T(8,128)(2,1)S(1)}, u32[]{:S(2)}, u32[]{:S(2)}) %collective-permute-start) | collective-permute-done | bytes 61472 | tf_op jit(solution)/shard_map/ppermute | solution.py:16
  13.2 3.5 %collective-permute-start.3 = (bf16[16,1920]{1,0:T(8,128)(2,1)S(1)}, bf16[16,1920]{1,0:T(8,128)(2,1)S(1)}, u32[]{:S(2)}, u32[]{:S(2)}) collective-permute-start(bf16[16,1920]{1,0:T(8,128)(2,1)S(1)} %collective-permute-done.1), channel_id=1, source_target_pairs={{0,25},{1,0},{8,1},{9,8},{16,9},{17,16},{24,17},{25,24},{2,27},{3,... | collective-permute-start | bytes 184328 | tf_op jit(solution)/shard_map/ppermute | solution.py:19
  16.7 2.0 %collective-permute-done.2 = bf16[16,1920]{1,0:T(8,128)(2,1)S(1)} collective-permute-done((bf16[16,1920]{1,0:T(8,128)(2,1)S(1)}, bf16[16,1920]{1,0:T(8,128)(2,1)S(1)}, u32[]{:S(2)}, u32[]{:S(2)}) %collective-permute-start.2) | collective-permute-done | bytes 61472 | tf_op jit(solution)/shard_map/ppermute | solution.py:16
  18.7 0.2 collective-permute-done.3
  18.9 3.8 %collective-permute-start.5 = (bf16[16,1920]{1,0:T(8,128)(2,1)S(1)}, bf16[16,1920]{1,0:T(8,128)(2,1)S(1)}, u32[]{:S(2)}, u32[]{:S(2)}) collective-permute-start(bf16[16,1920]{1,0:T(8,128)(2,1)S(1)} %collective-permute-done.3), channel_id=1, source_target_pairs={{0,25},{1,0},{8,1},{9,8},{16,9},{17,16},{24,17},{25,24},{2,27},{3,... | collective-permute-start | bytes 184328 | tf_op jit(solution)/shard_map/ppermute | solution.py:19
  22.8 1.4 %collective-permute-done.4 = bf16[16,1920]{1,0:T(8,128)(2,1)S(1)} collective-permute-done((bf16[16,1920]{1,0:T(8,128)(2,1)S(1)}, bf16[16,1920]{1,0:T(8,128)(2,1)S(1)}, u32[]{:S(2)}, u32[]{:S(2)}) %collective-permute-start.4) | collective-permute-done | bytes 61472 | tf_op jit(solution)/shard_map/ppermute | solution.py:16
  24.2 0.4 collective-permute-done.5
  24.6 5.0 %collective-permute-done.6 = bf16[16,1920]{1,0:T(8,128)(2,1)S(1)} collective-permute-done((bf16[16,1920]{1,0:T(8,128)(2,1)S(1)}, bf16[16,1920]{1,0:T(8,128)(2,1)S(1)}, u32[]{:S(2)}, u32[]{:S(2)}) %collective-permute-start.6) | collective-permute-done | bytes 61472 | tf_op jit(solution)/shard_map/ppermute | solution.py:16
  29.6 3.6 %fusion.4 = f32[128,1024]{1,0:T(8,128)} fusion(bf16[128,1920]{1,0:T(8,128)(2,1)S(1)} %constant_dynamic-update-slice_fusion, bf16[1,1920,1024]{2,1,0:T(8,128)(2,1)} %param.7), kind=kOutput, calls=%fused_computation.7 | convolution fusion | flops 503316480 | bytes 4947968 | tf_op jit(solution)/shard_map/dot_general | solution.py:72
  33.3 2.1 %copy.22 = bf16[32,8,32,128]{3,2,1,0:T(8,128)(2,1)S(1)} copy(bf16[32,8,32,128]{3,1,2,0:T(8,128)(2,1)} %bitcast.48) | data formatting | bytes 4194304
  35.5 22.1 %reduce-scatter.2.cloned.1.call-done = f32[32,1024]{1,0:T(8,128)} async-done(((f32[128,1024]{1,0:T(8,128)}), f32[32,1024]{1,0:T(8,128)}) %reduce-scatter.2.cloned.1.call-update) | async-done | bytes 131088 | tf_op jit(solution)/shard_map/reduce_scatter | solution.py:85
  57.6 1.0 %reshape.53 = f32[32,4,2,128]{3,2,1,0:T(2,128)S(1)} reshape(f32[32,1024]{1,0:T(8,128)} %reduce-scatter.2.cloned.1.call-done) | data formatting | bytes 262144 | tf_op jit(solution)/shard_map/reshape | solution.py:28
  58.8 0.1 multiply_reduce_fusion
  59.0 8.6 %all_gather.6 = bf16[128,4,128]{2,0,1:T(8,128)(2,1)S(1)} all-gather(bf16[32,4,128]{2,0,1:T(8,128)(2,1)S(1)} %multiply_convert_fusion), channel_id=1, replica_groups=mesh['section'=4,'seq'=4,'tp'=2] {'seq'}, dimensions={0}, use_global_device_ids=true | all-gather | bytes 163840 | tf_op jit(solution)/shard_map/all_gather | solution.py:90
  67.6 1.5 %bitcast_reduce_fusion = (f32[256,4,8]{0,2,1:T(8,128)S(1)}, f32[4,128,256,8]{2,1,3,0:T(8,128)S(1)}) fusion(bf16[256,4,8,128]{3,2,1,0:T(8,128)(2,1)S(1)} %bitcast.47, bf16[128,4,128]{2,0,1:T(8,128)(2,1)S(1)} %all_gather.6), kind=kOutput, calls=%fused_computation.5 | convolution fusion | flops 270524416 | bytes 6455296 | tf_op jit(solution)/shard_map/while/body/eval_jaxpr/tigd,rid->tigr/dot_general | solution.py:50
  69.1 1.9 %copy-done = f32[4,128,256,8]{2,1,3,0:T(8,128)} copy-done((f32[4,128,256,8]{2,1,3,0:T(8,128)}, f32[4,128,256,8]{2,1,3,0:T(8,128)S(1)}, u32[]{:S(2)}) %copy-start) | copy-done | bytes 4194328
  71.0 0.8 fusion.6
  71.9 7.3 %all-gather = bf16[128,4,1,128]{3,1,2,0:T(4,128)(2,1)S(1)} all-gather(bf16[32,4,1,128]{3,1,2,0:T(4,128)(2,1)S(1)} %copy.31), channel_id=2, replica_groups=mesh['section'=4,'seq'=4,'tp'=2] {'seq'}, dimensions={0}, use_global_device_ids=true | all-gather | bytes 163840 | tf_op jit(solution)/shard_map/all_gather | solution.py:91
  79.2 0.1 copy.14
  79.4 3.6 %fusion.2 = bf16[256,4,8,128]{0,3,2,1:T(8,128)(2,1)S(1)} fusion(f32[4,128,256,8]{2,1,3,0:T(8,128)} %copy-done, f32[4,8]{1,0:T(4,128)S(1)} %tanh.11, f32[256,4,8]{0,2,1:T(8,128)S(1)} %get-tuple-element.18, f32[256,4,8]{0,2,1:T(8,128)S(1)} %broadcast_maximum_fusion, f32[256,4,8]{0,2,1:T(8,128)S(1)} %get-tuple-element.17, bf16[128,4,1,128]{0,3,1,2:T(8,128)(2,1)S(1)} %copy.14), kind=kOutput, calls=%fused_computation.3 | convolution fusion | flops 275775488 | bytes 6520960 | tf_op jit(solution)/shard_map/while/body/eval_jaxpr/tigr,rid->tigd/dot_general | solution.py:57
  82.9 2.9 %copy.16 = bf16[1,256,4096]{2,1,0:T(8,128)(2,1)} copy(bf16[1,256,4096]{1,2,0:T(8,128)(2,1)S(1)} %bitcast.49) | data formatting | bytes 4194304 | tf_op jit(solution)/shard_map/convert_element_type | solution.py:96
  (28 shorter events, 0.6 us)
Async XLA Ops:
  6.5 51.1 %reduce-scatter.2.cloned.1.call-start = ((), (), s32[]{:S(2)}) async-start(), calls=%async_computation.1 | async-start | bytes 655360 | tf_op jit(solution)/shard_map/reduce_scatter | solution.py:85
  6.5 6.6 %collective-permute-start = (bf16[16,1920]{1,0:T(8,128)(2,1)}, bf16[16,1920]{1,0:T(8,128)(2,1)S(1)}, u32[]{:S(2)}, u32[]{:S(2)}) collective-permute-start(bf16[16,1920]{1,0:T(8,128)(2,1)} %param.6), channel_id=1, source_target_pairs={{0,1},{1,8},{8,9},{9,16},{16,17},{17,24},{24,25},{25,0},{2,3},{3,1... | collective-permute-start | bytes 184328 | tf_op jit(solution)/shard_map/ppermute | solution.py:16
  7.0 6.2 %collective-permute-start.1 = (bf16[16,1920]{1,0:T(8,128)(2,1)}, bf16[16,1920]{1,0:T(8,128)(2,1)S(1)}, u32[]{:S(2)}, u32[]{:S(2)}) collective-permute-start(bf16[16,1920]{1,0:T(8,128)(2,1)} %param.6), channel_id=1, source_target_pairs={{0,25},{1,0},{8,1},{9,8},{16,9},{17,16},{24,17},{25,24},{2,27},{3,... | collective-permute-start | bytes 184328 | tf_op jit(solution)/shard_map/ppermute | solution.py:19
  13.2 5.5 %collective-permute-start.2 = (bf16[16,1920]{1,0:T(8,128)(2,1)S(1)}, bf16[16,1920]{1,0:T(8,128)(2,1)S(1)}, u32[]{:S(2)}, u32[]{:S(2)}) collective-permute-start(bf16[16,1920]{1,0:T(8,128)(2,1)S(1)} %collective-permute-done), channel_id=1, source_target_pairs={{0,1},{1,8},{8,9},{9,16},{16,17},{17,24},{24,25},{25,0},{2,3},{3,1... | collective-permute-start | bytes 184328 | tf_op jit(solution)/shard_map/ppermute | solution.py:16
  13.2 5.7 %collective-permute-start.3 = (bf16[16,1920]{1,0:T(8,128)(2,1)S(1)}, bf16[16,1920]{1,0:T(8,128)(2,1)S(1)}, u32[]{:S(2)}, u32[]{:S(2)}) collective-permute-start(bf16[16,1920]{1,0:T(8,128)(2,1)S(1)} %collective-permute-done.1), channel_id=1, source_target_pairs={{0,25},{1,0},{8,1},{9,8},{16,9},{17,16},{24,17},{25,24},{2,27},{3,... | collective-permute-start | bytes 184328 | tf_op jit(solution)/shard_map/ppermute | solution.py:19
  18.7 5.4 %collective-permute-start.4 = (bf16[16,1920]{1,0:T(8,128)(2,1)S(1)}, bf16[16,1920]{1,0:T(8,128)(2,1)S(1)}, u32[]{:S(2)}, u32[]{:S(2)}) collective-permute-start(bf16[16,1920]{1,0:T(8,128)(2,1)S(1)} %collective-permute-done.2), channel_id=1, source_target_pairs={{0,1},{1,8},{8,9},{9,16},{16,17},{17,24},{24,25},{25,0},{2,3},{3,1... | collective-permute-start | bytes 184328 | tf_op jit(solution)/shard_map/ppermute | solution.py:16
  18.9 5.7 %collective-permute-start.5 = (bf16[16,1920]{1,0:T(8,128)(2,1)S(1)}, bf16[16,1920]{1,0:T(8,128)(2,1)S(1)}, u32[]{:S(2)}, u32[]{:S(2)}) collective-permute-start(bf16[16,1920]{1,0:T(8,128)(2,1)S(1)} %collective-permute-done.3), channel_id=1, source_target_pairs={{0,25},{1,0},{8,1},{9,8},{16,9},{17,16},{24,17},{25,24},{2,27},{3,... | collective-permute-start | bytes 184328 | tf_op jit(solution)/shard_map/ppermute | solution.py:19
  24.2 5.4 %collective-permute-start.6 = (bf16[16,1920]{1,0:T(8,128)(2,1)S(1)}, bf16[16,1920]{1,0:T(8,128)(2,1)S(1)}, u32[]{:S(2)}, u32[]{:S(2)}) collective-permute-start(bf16[16,1920]{1,0:T(8,128)(2,1)S(1)} %collective-permute-done.4), channel_id=1, source_target_pairs={{0,1},{1,8},{8,9},{9,16},{16,17},{17,24},{24,25},{25,0},{2,3},{3,1... | collective-permute-start | bytes 184328 | tf_op jit(solution)/shard_map/ppermute | solution.py:16
  29.6 5.8 %copy-start.2 = (f32[1,32]{1,0:T(1,128)S(1)}, f32[1,32]{1,0:T(1,128)}, u32[]{:S(2)}) copy-start(f32[1,32]{1,0:T(1,128)} %param.9) | copy-start | bytes 388
  29.6 29.3 %copy-start.1 = (f32[1,128]{1,0:T(1,128)S(1)}, f32[1,128]{1,0:T(1,128)}, u32[]{:S(2)}) copy-start(f32[1,128]{1,0:T(1,128)} %param.8) | copy-start | bytes 1540
  69.1 1.9 %copy-start = (f32[4,128,256,8]{2,1,3,0:T(8,128)}, f32[4,128,256,8]{2,1,3,0:T(8,128)S(1)}, u32[]{:S(2)}) copy-start(f32[4,128,256,8]{2,1,3,0:T(8,128)S(1)} %get-tuple-element.20) | copy-start | bytes 12582916
Sparse Core Ops, SparseCore 0:
  33.4 24.1 reduce-scatter.1
